TPU v7x, 256 devices: a whole 4x4x8 slice. The times are simulated.
256 devices in a mesh: section: 16 (over y_hi, x, core), ray: 8 (over z), dp: 2 (over y_lo).
Axes of the slice: x: 4, y: 4 (y_hi: 2, y_lo: 2; y = y_hi * 2 + y_lo), z: 8, core: 2. Of those that a mesh axis runs over, the one named last changes fastest.
Arguments:
- section_tokens: bfloat16 [16, 2, 1024, 1024], P('section', 'dp', 'ray'), may hold values from -6 to 6
- enc_ln1: float32 [16, 1024], P('section'), may hold values from 0.5 to 1.5
- enc_qkv: bfloat16 [16, 1024, 3, 1024], P('section', None, None, 'ray'), may hold values from -40 to 40
- enc_out: bfloat16 [16, 1024, 1024], P('section', 'ray'), may hold values from -0.1875 to 0.1875
- enc_ln2: float32 [16, 1024], P('section'), may hold values from 0.5 to 1.5
- enc_up: bfloat16 [16, 1024, 4096], P('section', None, 'ray'), may hold values from -0.1875 to 0.1875
- enc_down: bfloat16 [16, 4096, 1024], P('section', 'ray'), may hold values from -0.09375 to 0.09375
- set_latent: bfloat16 [2, 1024, 1024], P('dp', 'ray'), may hold values from -6 to 6
- ray_queries: bfloat16 [2, 32768, 1024], P('dp', ('section', 'ray')), may hold values from -6 to 6
- dec_query: bfloat16 [1024, 1024], P('section'), may hold values from -40 to 40
- dec_kv: bfloat16 [1024, 2, 1024], P('section'), may hold values from -1 to 1
- dec_out: bfloat16 [1024, 1024], P('section'), may hold values from -0.1875 to 0.1875
- feature_grad: bfloat16 [2, 32768, 1024], P('dp', ('section', 'ray')), may hold values from -2 to 2
Outputs:
- handed: bfloat16 [16, 2, 1024, 1024], P('section', 'dp', 'ray')
- finished: bfloat16 [2, 1024, 1024], P('dp', 'ray', 'section')
- ray_features: bfloat16 [2, 32768, 1024], P('dp', ('section', 'ray'))
- latent_grad: bfloat16 [2, 1024, 1024], P('dp', 'ray')
- out_grad: float32 [1024, 1024], replicated
All inputs are finite; a program needn't handle non-finite values.
Results may differ from a plain program's by a relative error of at most 0.022.
The roundings to bfloat16 on the way count: a program that leaves them out, or rounds other values in their place, can miss the bound.
Values may be sent and summed in bfloat16 or wider, within the bound.
No kernel may reach another device: no remote copies, remote signals or barrier semaphores. Data moves between devices by JAX's collectives and lax.ppermute only.
A program may use at most 128 MiB of HBM per device.

v0:
```python
import math

import jax
import jax.numpy as jnp
from jax import lax
from jax.sharding import PartitionSpec as P

HEADS = 16


def shifted(value, axis, by):
    count = lax.axis_size(axis)
    pairs = [(i, i + by) for i in range(count) if 0 <= i + by < count]
    return lax.ppermute(value, axis, pairs)


def spread_2(value, axis, root):
    mine = lax.axis_index(axis) == root
    return lax.psum(jnp.where(mine, value, jnp.zeros_like(value)), axis)


def layer_norm(values, gain):
    values = values.astype(jnp.float32)
    center = values - jnp.mean(values, -1, keepdims=True)
    spread = jnp.mean(center * center, -1, keepdims=True)
    return center * lax.rsqrt(spread + 1e-05) * gain


def softmax_rows(scores):
    top = jnp.max(scores, -1, keepdims=True)
    expo = jnp.exp(scores - top)
    return expo / jnp.sum(expo, -1, keepdims=True)


def attend_heads(packed, head_dim):
    length = packed.shape[0]
    heads = packed.shape[1] // (3 * head_dim)
    split = packed.reshape(length, 3, heads, head_dim)
    scores = jnp.einsum(
        "qhd,khd->hqk", split[:, 0], split[:, 1], preferred_element_type=jnp.float32
    ) / math.sqrt(head_dim)
    probs = softmax_rows(scores).astype(jnp.bfloat16)
    mixed = jnp.einsum("hqk,khd->qhd", probs, split[:, 2], preferred_element_type=jnp.float32)
    return mixed.astype(jnp.bfloat16).reshape(length, heads * head_dim)


def latent_rows(pair_sum, w_pairs):
    result = lax.dot_general(
        pair_sum[:, 0],
        w_pairs[:, 0, :],
        (((1,), (1,)), ((), ())),
        preferred_element_type=jnp.float32,
    )
    result = result + lax.dot_general(
        pair_sum[:, 1],
        w_pairs[:, 1, :],
        (((1,), (1,)), ((), ())),
        preferred_element_type=jnp.float32,
    )
    return result.astype(jnp.bfloat16)


def local(
    section_tokens,
    enc_ln1,
    enc_qkv,
    enc_out,
    enc_ln2,
    enc_up,
    enc_down,
    set_latent,
    ray_queries,
    dec_query,
    dec_kv,
    dec_out,
    feature_grad,
):
    tokens = section_tokens[0, 0]
    width = tokens.shape[1]
    head_dim = width // HEADS
    local_width = enc_out.shape[1]
    w_qkv = enc_qkv[0].reshape(width, 3 * local_width)
    w_attn_out = enc_out[0]
    w_upper = enc_up[0]
    w_lower = enc_down[0]
    gain_one = enc_ln1[0]
    gain_two = enc_ln2[0]
    normed = layer_norm(tokens, gain_one).astype(jnp.bfloat16)
    packed = jnp.dot(
        lax.all_gather(normed, "ray", axis=0, tiled=True), w_qkv, preferred_element_type=jnp.float32
    ).astype(jnp.bfloat16)
    mixed = attend_heads(packed, head_dim)
    attn_rows = lax.psum_scatter(
        jnp.dot(mixed, w_attn_out, preferred_element_type=jnp.float32).astype(jnp.bfloat16),
        "ray",
        scatter_dimension=0,
        tiled=True,
    ).astype(jnp.float32)
    hidden = (tokens.astype(jnp.float32) + attn_rows).astype(jnp.bfloat16)
    upper = jax.nn.gelu(
        jnp.dot(
            lax.all_gather(
                layer_norm(hidden, gain_two).astype(jnp.bfloat16), "ray", axis=0, tiled=True
            ),
            w_upper,
            preferred_element_type=jnp.float32,
        ),
        approximate=True,
    ).astype(jnp.bfloat16)
    lower_rows = lax.psum_scatter(
        jnp.dot(upper, w_lower, preferred_element_type=jnp.float32).astype(jnp.bfloat16),
        "ray",
        scatter_dimension=0,
        tiled=True,
    ).astype(jnp.float32)
    layer_out = (hidden.astype(jnp.float32) + lower_rows).astype(jnp.bfloat16)
    handed = shifted(layer_out, "section", 1)
    finished_all = spread_2(layer_out, "section", lax.axis_size("section") - 1)
    columns = width // lax.axis_size("section")
    finished = lax.dynamic_slice_in_dim(
        finished_all, lax.axis_index("section") * columns, columns, 1
    )
    w_query, w_pairs, w_mix = (
        lax.all_gather(dec_query, "section", axis=0, tiled=True),
        lax.all_gather(dec_kv, "section", axis=0, tiled=True),
        lax.all_gather(dec_out, "section", axis=0, tiled=True),
    )
    latent = set_latent[0]
    queries = ray_queries[0]
    cotangent = feature_grad[0]
    flat_pairs = w_pairs.reshape(width, 2 * width)
    key_values = lax.all_gather(
        jnp.dot(latent, flat_pairs, preferred_element_type=jnp.float32).astype(jnp.bfloat16),
        "ray",
        axis=0,
        tiled=True,
    )
    scene_len = key_values.shape[0]
    ray_rows = queries.shape[0]
    scale = 1.0 / math.sqrt(head_dim)
    keys = key_values[:, :width].reshape(scene_len, HEADS, head_dim)
    values = key_values[:, width:].reshape(scene_len, HEADS, head_dim)
    query = (
        jnp.dot(queries, w_query, preferred_element_type=jnp.float32)
        .astype(jnp.bfloat16)
        .reshape(ray_rows, HEADS, head_dim)
    )
    scores = jnp.einsum("rhd,lhd->hrl", query, keys, preferred_element_type=jnp.float32) * scale
    probs = softmax_rows(scores)
    probs_low = probs.astype(jnp.bfloat16)
    attended = (
        jnp.einsum("hrl,lhd->rhd", probs_low, values, preferred_element_type=jnp.float32)
        .astype(jnp.bfloat16)
        .reshape(ray_rows, width)
    )
    features = (
        queries.astype(jnp.float32) + jnp.dot(attended, w_mix, preferred_element_type=jnp.float32)
    ).astype(jnp.bfloat16)
    mix_term = lax.dot_general(
        attended, cotangent, (((0,), (0,)), ((), ())), preferred_element_type=jnp.float32
    )
    out_grad = lax.psum(mix_term, ("section", "ray", "dp"))
    attn_grad = lax.dot_general(
        cotangent, w_mix, (((1,), (1,)), ((), ())), preferred_element_type=jnp.float32
    )
    attn_grad = attn_grad.astype(jnp.bfloat16).reshape(ray_rows, HEADS, head_dim)
    prob_grad = jnp.einsum("rhd,lhd->hrl", attn_grad, values, preferred_element_type=jnp.float32)
    delta = jnp.sum(probs * prob_grad, -1, keepdims=True)
    score_grad = (probs * (prob_grad - delta) * scale).astype(jnp.bfloat16)
    count = latent.shape[0] * lax.axis_size("ray")
    key_grad = jnp.einsum(
        "hrl,rhd->lhd", score_grad, query, preferred_element_type=jnp.float32
    ).reshape(count, width)
    value_grad = jnp.einsum(
        "hrl,rhd->lhd", probs_low, attn_grad, preferred_element_type=jnp.float32
    ).reshape(count, width)
    stacked = jnp.stack([key_grad, value_grad], 1)
    pair_rows = lax.psum_scatter(
        stacked.astype(jnp.bfloat16), "ray", scatter_dimension=0, tiled=True
    )
    pair_sum = lax.psum(pair_rows, "section")
    latent_grad = latent_rows(pair_sum, w_pairs)
    return (handed[None, None], finished[None], features[None], latent_grad[None], out_grad)


def solution(mesh):
    return jax.shard_map(
        local,
        mesh=mesh,
        in_specs=(
            P("section", "dp", "ray", None),
            P("section", None),
            P("section", None, None, "ray"),
            P("section", "ray", None),
            P("section", None),
            P("section", None, "ray"),
            P("section", "ray", None),
            P("dp", "ray", None),
            P("dp", ("section", "ray"), None),
            P("section", None),
            P("section", None, None),
            P("section", None),
            P("dp", ("section", "ray"), None),
        ),
        out_specs=(
            P("section", "dp", "ray", None),
            P("dp", "ray", "section"),
            P("dp", ("section", "ray"), None),
            P("dp", "ray", None),
            P(),
        ),
        check_vma=False,
    )
```

profile of v0, /device:TPU:2, one launch (start us, length us, event | category | flops | bytes accessed | tf_op | source)
XLA Modules:
  0.0 928.3 jit_solution(4946242236666145838)
XLA Ops:
  8.1 1.1 convert_reduce_fusion.1
  9.2 1.2 fusion.73
  10.4 1.9 fusion.75
  12.3 0.0 reduce-scatter.6.cloned.1.call-start
  12.4 1.4 copy.44
  13.8 42.5 %all-gather.7.cloned.1.call-done = bf16[1024,1024]{1,0:T(8,128)(2,1)} async-done(((bf16[128,1024]{1,0:T(8,128)(2,1)}), bf16[1024,1024]{1,0:T(8,128)(2,1)}) %all-gather.7.cloned.1.call-update) | async-done | bytes 2097168 | tf_op jit(solution)/shard_map/all_gather | solution.py:90
  56.3 2.6 convolution_convert_fusion.3
  58.9 4.9 fusion.97
  63.7 4.3 fusion.48
  68.1 2.1 convolution_convert_fusion.2
  70.1 0.0 all-gather.11.cloned.1.call-start
  70.2 0.5 all-gather.11.cloned.1.call-update
  70.7 0.0 all-gather.15.cloned.1.call-start
  70.8 0.5 all-gather.15.cloned.1.call-update
  71.3 0.0 all-gather.17.cloned.1.call-start
  71.4 0.5 all-gather.17.cloned.1.call-update
  71.9 0.0 all-gather.9.cloned.1.call-start
  71.9 39.7 %reduce-scatter.6.cloned.1.call-done = bf16[128,1024]{1,0:T(8,128)(2,1)} async-done(((bf16[1024,1024]{1,0:T(8,128)(2,1)}), bf16[128,1024]{1,0:T(8,128)(2,1)}) %reduce-scatter.6.cloned.1.call-update) | async-done | bytes 262160 | tf_op jit(solution)/shard_map/reduce_scatter | solution.py:93
  111.7 1.1 convert_reduce_fusion
  112.8 0.2 fusion.70
  113.0 0.9 fusion.72
  114.0 0.0 all-gather.13.cloned.1.call-start
  114.0 18.6 %all-gather.11.cloned.1.call-done = bf16[1024,2,1024]{2,1,0:T(2,128)(2,1)} async-done(((bf16[64,2,1024]{2,1,0:T(2,128)(2,1)}), bf16[1024,2,1024]{2,1,0:T(2,128)(2,1)}) %all-gather.11.cloned.1.call-update) | async-done | bytes 4194320 | tf_op jit(solution)/shard_map/all_gather | solution.py:125
  132.7 11.1 %copy.47 = bf16[1024,2,1024]{0,2,1:T(8,128)(2,1)} copy(bf16[1024,2,1024]{2,1,0:T(2,128)(2,1)} %all-gather.11.cloned.1.call-done) | data formatting | bytes 8388608 | tf_op jit(solution)/shard_map/all_gather | solution.py:125
  143.8 4.6 convolution_convert_fusion
  148.5 0.0 reduce-scatter.8.cloned.1.call-start
  148.5 39.0 %all-gather.15.cloned.1.call-done = bf16[1024,1024]{1,0:T(8,128)(2,1)} async-done(((bf16[64,1024]{1,0:T(8,128)(2,1)}), bf16[1024,1024]{1,0:T(8,128)(2,1)}) %all-gather.15.cloned.1.call-update) | async-done | bytes 2097168 | tf_op jit(solution)/shard_map/all_gather | solution.py:124
  187.5 2.3 convolution_convert_fusion.5
  189.8 1.0 copy.49
  190.8 51.5 %all-gather.17.cloned.1.call-done = bf16[1024,1024]{1,0:T(8,128)(2,1)} async-done(((bf16[64,1024]{1,0:T(8,128)(2,1)}), bf16[1024,1024]{1,0:T(8,128)(2,1)}) %all-gather.17.cloned.1.call-update) | async-done | bytes 2097168 | tf_op jit(solution)/shard_map/all_gather | solution.py:126
  242.3 2.3 convolution_convert_fusion.4
  244.6 1.0 copy.51
  245.6 39.2 %all-gather.9.cloned.1.call-done = bf16[1024,1024]{1,0:T(8,128)(2,1)} async-done(((bf16[128,1024]{1,0:T(8,128)(2,1)}), bf16[1024,1024]{1,0:T(8,128)(2,1)}) %all-gather.9.cloned.1.call-update) | async-done | bytes 2097168 | tf_op jit(solution)/shard_map/all_gather | solution.py:102
  284.9 5.8 convolution_convert_fusion.1
  290.7 0.2 reduce-scatter.10.cloned.1.call-start
  290.9 66.2 %all-gather.13.cloned.1.call-done = bf16[1024,2048]{1,0:T(8,128)(2,1)} async-done(((bf16[128,2048]{1,0:T(8,128)(2,1)}), bf16[1024,2048]{1,0:T(8,128)(2,1)}) %all-gather.13.cloned.1.call-update) | async-done | bytes 4194320 | tf_op jit(solution)/shard_map/all_gather | solution.py:132
  357.2 4.0 fusion.96
  361.2 2.6 copy.50
  363.8 2.9 copy.48
  366.7 9.8 %fusion.98 = (f32[16,256]{1,0:T(8,128)S(1)}, f32[16,256,1024]{2,1,0:T(8,128)}) fusion(bf16[256,16,64]{0,2,1:T(8,128)(2,1)S(1)} %bitcast.149, bf16[1024,16,64]{0,2,1:T(8,128)(2,1)} %bitcast.144), kind=kOutput, calls=%fused_computation.110 | convolution fusion | flops 549454848 | bytes 19415040 | tf_op jit(solution)/shard_map/sub | solution.py:31
  376.5 8.1 fusion.99
  384.5 38.2 %fusion.38 = bf16[16,64,1024]{2,1,0:T(8,128)(2,1)} fusion(bf16[256,16,64]{0,2,1:T(8,128)(2,1)S(1)} %bitcast.150, f32[16,256,1024]{2,1,0:T(8,128)} %fusion.99, f32[16,256,1024]{2,1,0:T(8,128)} %get-tuple-element.18, f32[16,256]{1,0:T(8,128)S(1)} %get-tuple-element.17), kind=kOutput, calls=%fused_computation.40 | convolution fusion | flops 567284736 | bytes 36192256 | tf_op jit(solution)/shard_map/hrl,rhd->lhd/dot_general | solution.py:171
  422.8 7.1 fusion.35
  429.9 2.4 pad_maximum_fusion
  432.3 6.5 copy.57
  438.8 0.0 all-reduce.6.cloned.1.call-start
  438.9 1.9 broadcast_select_fusion
  440.8 52.2 %reduce-scatter.10.cloned.1.call-done = bf16[128,2048]{1,0:T(8,128)(2,1)} async-done(((bf16[1024,2048]{1,0:T(8,128)(2,1)}), bf16[128,2048]{1,0:T(8,128)(2,1)}) %reduce-scatter.10.cloned.1.call-update) | async-done | bytes 524304
  492.9 2.0 copy.58
  495.0 0.3 all-reduce.4.cloned.1.call-start
  495.3 8.5 fusion.42
  503.8 2.7 fusion.78
  506.5 10.0 %fusion.95 = (bf16[1024,1,1024]{2,1,0:T(2,128)(2,1)}, bf16[1024,1,1024]{2,1,0:T(2,128)(2,1)}) fusion(bf16[1024,2,1024]{2,1,0:T(2,128)(2,1)} %all-gather.11.cloned.1.call-done), kind=kLoop, calls=%fused_computation.107 | loop fusion | bytes 8388608 | tf_op jit(solution)/shard_map/slice | solution.py:50
  516.5 1.9 collective-permute-start
  518.5 1.5 fusion.45
  520.0 4.7 collective-permute-done
  524.7 109.9 %all-reduce.6.cloned.1.call-done = (bf16[128,1024]{1,0:T(8,128)(2,1)}, bf16[128,2,1024]{0,2,1:T(8,128)(2,1)}) async-done(((bf16[128,1024]{1,0:T(8,128)(2,1)}, bf16[128,2,1024]{0,2,1:T(8,128)(2,1)}), (bf16[128,1024]{1,0:T(8,128)(2,1)}, bf16[128,2,1024]{0,2,1:T(8,128)(2,1)})) %all-reduce.6.cloned.1.call-update) | async-done | bytes 786448 | tf_op jit(solution)/shard_map/psum | solution.py:19
  634.6 0.8 constant_dynamic-slice_fusion
  635.5 0.7 copy.46
  636.2 3.1 fusion.33
  639.3 3.9 fusion.49
  643.2 272.5 %all-reduce.4.cloned.1.call-done = f32[1024,1024]{1,0:T(8,128)} async-done(((f32[1024,1024]{1,0:T(8,128)}), f32[1024,1024]{1,0:T(8,128)}) %all-reduce.4.cloned.1.call-update) | async-done | bytes 4194320 | tf_op jit(solution)/shard_map/psum | solution.py:162
  915.7 0.7 copy.75
  916.4 4.8 copy.76
  (44 shorter events, 0.3 us)
Async XLA Ops:
  8.0 276.9 %copy-start = (bf16[1,512,1024]{2,1,0:T(8,128)(2,1)S(1)}, bf16[1,512,1024]{2,1,0:T(8,128)(2,1)}, u32[]{:S(2)}) copy-start(bf16[1,512,1024]{2,1,0:T(8,128)(2,1)} %param.19) | copy-start | bytes 3145732
  8.0 48.2 %all-gather.7.cloned.1.call-start = ((), (), s32[]{:S(2)}) async-start(), calls=%async_computation.3 | async-start | bytes 2359296 | tf_op jit(solution)/shard_map/all_gather | solution.py:90
  12.3 99.4 %reduce-scatter.6.cloned.1.call-start = ((), (), s32[]{:S(2)}) async-start(), calls=%async_computation.4 | async-start | bytes 2359296 | tf_op jit(solution)/shard_map/reduce_scatter | solution.py:93
  63.7 4.3 copy-start.11
  68.0 43.6 %copy-start.2 = (bf16[1,1,128,1024]{3,2,1,0:T(8,128)(2,1)S(1)}, bf16[1,1,128,1024]{3,2,1,0:T(8,128)(2,1)}, u32[]{:S(2)}) copy-start(bf16[1,1,128,1024]{3,2,1,0:T(8,128)(2,1)} %param.13) | copy-start | bytes 786436
  68.0 45.0 %copy-start.14 = (f32[1,1024]{1,0:T(1,128)S(1)}, f32[1,1024]{1,0:T(1,128)}, u32[]{:S(2)}) copy-start(f32[1,1024]{1,0:T(1,128)} %param.17) | copy-start | bytes 12292
  70.1 62.5 %all-gather.11.cloned.1.call-start = ((), (), s32[]{:S(2)}) async-start(), calls=%async_computation.7 | async-start | bytes 4456448 | tf_op jit(solution)/shard_map/all_gather | solution.py:125
  70.7 116.8 %all-gather.15.cloned.1.call-start = ((), (), s32[]{:S(2)}) async-start(), calls=%async_computation.9 | async-start | bytes 2228224 | tf_op jit(solution)/shard_map/all_gather | solution.py:124
  71.3 171.0 %all-gather.17.cloned.1.call-start = ((), (), s32[]{:S(2)}) async-start(), calls=%async_computation.10 | async-start | bytes 2228224 | tf_op jit(solution)/shard_map/all_gather | solution.py:126
  71.9 213.0 %all-gather.9.cloned.1.call-start = ((), (), s32[]{:S(2)}) async-start(), calls=%async_computation.5 | async-start | bytes 2359296 | tf_op jit(solution)/shard_map/all_gather | solution.py:102
  114.0 29.8 %copy-start.12 = (bf16[1,128,1024]{2,1,0:T(8,128)(2,1)S(1)}, bf16[1,128,1024]{2,1,0:T(8,128)(2,1)}, u32[]{:S(2)}) copy-start(bf16[1,128,1024]{2,1,0:T(8,128)(2,1)} %param.20) | copy-start | bytes 786436
  114.0 243.2 %all-gather.13.cloned.1.call-start = ((), (), s32[]{:S(2)}) async-start(), calls=%async_computation.8 | async-start | bytes 4718592 | tf_op jit(solution)/shard_map/all_gather | solution.py:132
  143.8 43.7 %copy-start.8 = (bf16[1,256,1024]{2,1,0:T(8,128)(2,1)S(1)}, bf16[1,256,1024]{2,1,0:T(8,128)(2,1)}, u32[]{:S(2)}) copy-start(bf16[1,256,1024]{2,1,0:T(8,128)(2,1)} %param.21) | copy-start | bytes 1572868
  143.8 98.5 %copy-start.6 = (bf16[1,256,1024]{2,1,0:T(8,128)(2,1)S(1)}, bf16[1,256,1024]{2,1,0:T(8,128)(2,1)}, u32[]{:S(2)}) copy-start(bf16[1,256,1024]{2,1,0:T(8,128)(2,1)} %param.25) | copy-start | bytes 1572868
  148.5 290.5 %reduce-scatter.8.cloned.1.call-start = ((), (), s32[]{:S(2)}) async-start(), calls=%async_computation.6 | async-start | bytes 2359296 | tf_op jit(solution)/shard_map/reduce_scatter | solution.py:110
  290.7 202.2 %reduce-scatter.10.cloned.1.call-start = ((), (), s32[]{:S(2)}) async-start(), calls=%async_computation.12 | async-start | bytes 4718592
  361.2 5.4 copy-start.10
  366.6 9.8 %copy-start.4 = (bf16[256,1024]{0,1:T(8,128)(2,1)S(1)}, bf16[256,1024]{0,1:T(8,128)(2,1)}, u32[]{:S(2)}) copy-start(bf16[256,1024]{0,1:T(8,128)(2,1)} %copy.51) | copy-start | bytes 1572868
  422.8 7.1 copy-start.5
  438.8 195.8 %all-reduce.6.cloned.1.call-start = ((), (), s32[]{:S(2)}) async-start(), calls=%async_computation.13 | async-start | bytes 1572864 | tf_op jit(solution)/shard_map/psum | solution.py:19
  495.0 8.8 copy-start.7
  495.0 420.7 %all-reduce.4.cloned.1.call-start = ((), (), s32[]{:S(2)}) async-start(), calls=%async_computation.11 | async-start | bytes 8388608 | tf_op jit(solution)/shard_map/psum | solution.py:162
  506.5 10.0 %copy-start.13 = (bf16[128,1024]{1,0:T(8,128)(2,1)S(1)}, bf16[128,1024]{1,0:T(8,128)(2,1)}, u32[]{:S(2)}) copy-start(bf16[128,1024]{1,0:T(8,128)(2,1)} %get-tuple-element.8) | copy-start | bytes 786436
  506.5 11.9 %copy-start.3 = (bf16[1024,1024]{1,0:T(8,128)(2,1)S(1)}, bf16[1024,1024]{1,0:T(8,128)(2,1)}, u32[]{:S(2)}) copy-start(bf16[1024,1024]{1,0:T(8,128)(2,1)} %all-gather.17.cloned.1.call-done) | copy-start | bytes 6291460
  506.5 11.9 %copy-start.9 = (bf16[1,256,1024]{2,1,0:T(8,128)(2,1)S(1)}, bf16[1,256,1024]{2,1,0:T(8,128)(2,1)}, u32[]{:S(2)}) copy-start(bf16[1,256,1024]{2,1,0:T(8,128)(2,1)} %param.21) | copy-start | bytes 1572868
  516.5 8.2 collective-permute-start
  915.7 5.5 copy-start.1
Sparse Core Ops, SparseCore 0:
  12.4 43.7 all-gather.6
  70.3 41.3 reduce-scatter.5
  290.8 69.1 reduce-scatter.7
  439.0 53.9 reduce-scatter.9
Sparse Core Ops, SparseCore 1:
  73.4 59.3 all-gather.10
  135.3 52.1 all-gather.14
  190.1 52.1 all-gather.16
  244.7 40.1 all-gather.8
  286.7 70.4 all-gather.12
  495.1 139.5 all-reduce.5
  640.0 275.7 all-reduce.3
where the time goes:
time: 929 us; the launch traced here: 928 us
  waiting for transfers between devices  738 us (79%)
  matrix products  112 us (12%)
  local copies, waits for them, and re-layouts  49.6 us (5%)
  between operations  15.6 us (2%)
  other arithmetic  10.7 us (1%)
    psum x1, waiting for transfers between devices, local(): out_grad = lax.psum(mix_term, ('section', 'ray', 'dp'))  273 us
    psum x1, waiting for transfers between devices, spread_2(): return lax.psum(jnp.where(mine, value, jnp.zeros_like(value)), axis)  110 us
    all_gather x1, waiting for transfers between devices, local(): lax.all_gather(jnp.dot(latent, flat_pairs, preferred_element_type=jnp.flo...  66.2 us
    unnamed x12, waiting for transfers between devices  53.9 us
    all_gather x1, waiting for transfers between devices, local(): lax.all_gather(dec_out, 'section', axis=0, tiled=True)  51.5 us
    all_gather x1, waiting for transfers between devices, local(): lax.all_gather(normed, 'ray', axis=0, tiled=True)  42.5 us
    reduce_scatter x1, waiting for transfers between devices, local(): lax.psum_scatter(jnp.dot(mixed, w_attn_out, preferred_element_type=jnp.fl...  39.7 us
    all_gather x1, waiting for transfers between devices, local(): lax.all_gather(layer_norm(hidden, gain_two).astype(jnp.bfloat16), 'ray',...  39.2 us
  transfers between devices with their start and end apart: 12, of which 11 were waited for; matrix products, arithmetic and copies ran while one was open for 16% of the time, Pallas kernels for 0%

commit v1 on v0

v1 whole, which is shorter than its diff:
```python
import math

import jax
import jax.numpy as jnp
from jax import lax
from jax.experimental import pallas as pl
from jax.experimental.pallas import tpu as pltpu
from jax.sharding import PartitionSpec as P

HEADS = 16


def shifted(value, axis, by):
    count = lax.axis_size(axis)
    pairs = [(i, i + by) for i in range(count) if 0 <= i + by < count]
    return lax.ppermute(value, axis, pairs)


def layer_norm(values, gain):
    values = values.astype(jnp.float32)
    center = values - jnp.mean(values, -1, keepdims=True)
    spread = jnp.mean(center * center, -1, keepdims=True)
    return center * lax.rsqrt(spread + 1e-05) * gain


def softmax_rows(scores):
    top = jnp.max(scores, -1, keepdims=True)
    expo = jnp.exp(scores - top)
    return expo / jnp.sum(expo, -1, keepdims=True)


def attend_heads(packed, head_dim):
    length = packed.shape[0]
    heads = packed.shape[1] // (3 * head_dim)
    split = packed.reshape(length, 3, heads, head_dim)
    scores = jnp.einsum(
        "qhd,khd->hqk", split[:, 0], split[:, 1], preferred_element_type=jnp.float32
    ) / math.sqrt(head_dim)
    probs = softmax_rows(scores).astype(jnp.bfloat16)
    mixed = jnp.einsum("hqk,khd->qhd", probs, split[:, 2], preferred_element_type=jnp.float32)
    return mixed.astype(jnp.bfloat16).reshape(length, heads * head_dim)


def exchange(blocks, axis):
    return lax.all_to_all(blocks, axis, split_axis=0, concat_axis=0, tiled=True)


def after(value, *others):
    return lax.optimization_barrier((value,) + others)[0]


def gather_small(value, axis):
    count = lax.axis_size(axis)
    return exchange(jnp.broadcast_to(value[None], (count,) + value.shape), axis)


NT = (((1,), (1,)), ((), ()))
TN = (((0,), (0,)), ((), ()))


def head_kernel(pairs_ref, rays_ref, mixed_ref, grads_ref, keys, values, values_t, key_sum, value_sum):
    step = pl.program_id(0)
    dim = keys.shape[1]
    scale = 1.0 / math.sqrt(dim)

    @pl.when(step == 0)
    def _():
        keys[...] = pairs_ref[:, :dim]
        values[...] = pairs_ref[:, dim:]
        values_t[...] = pairs_ref[:, dim:].T
        key_sum[...] = jnp.zeros_like(key_sum)
        value_sum[...] = jnp.zeros_like(value_sum)

    query = rays_ref[0, :dim, :]
    grad = rays_ref[0, dim:, :]
    scores = jnp.dot(keys[...], query, preferred_element_type=jnp.float32)
    top = jnp.max(scores, 0, keepdims=True)
    expo = jnp.exp((scores - top) * scale)
    probs = expo * (1.0 / jnp.sum(expo, 0, keepdims=True))
    low = probs.astype(jnp.bfloat16)
    mixed_ref[0] = jnp.dot(values_t[...], low, preferred_element_type=jnp.float32).astype(jnp.bfloat16)
    prob_grad = jnp.dot(values[...], grad, preferred_element_type=jnp.float32)
    delta = jnp.sum(probs * prob_grad, 0, keepdims=True)
    score_grad = (probs * (prob_grad - delta) * scale).astype(jnp.bfloat16)
    key_part = lax.dot_general(score_grad, query, NT, preferred_element_type=jnp.float32)
    value_part = lax.dot_general(low, grad, NT, preferred_element_type=jnp.float32)
    key_sum[...] += key_part.astype(jnp.bfloat16).astype(jnp.float32)
    value_sum[...] += value_part.astype(jnp.bfloat16).astype(jnp.float32)

    @pl.when(step == pl.num_programs(0) - 1)
    def _():
        grads_ref[:, :dim] = key_sum[...].astype(jnp.bfloat16)
        grads_ref[:, dim:] = value_sum[...].astype(jnp.bfloat16)


def attend_rays(pairs, rays):
    blocks, both, width = rays.shape
    length = pairs.shape[0]
    dim = both // 2
    work = blocks * width * length
    return pl.pallas_call(
        head_kernel,
        grid=(blocks,),
        in_specs=[
            pl.BlockSpec((length, both), lambda i: (0, 0)),
            pl.BlockSpec((1, both, width), lambda i: (i, 0, 0)),
        ],
        out_specs=[
            pl.BlockSpec((1, dim, width), lambda i: (i, 0, 0)),
            pl.BlockSpec((length, both), lambda i: (0, 0)),
        ],
        out_shape=[
            jax.ShapeDtypeStruct((blocks, dim, width), jnp.bfloat16),
            jax.ShapeDtypeStruct((length, both), jnp.bfloat16),
        ],
        scratch_shapes=[
            pltpu.VMEM((length, dim), jnp.bfloat16),
            pltpu.VMEM((length, dim), jnp.bfloat16),
            pltpu.VMEM((dim, length), jnp.bfloat16),
            pltpu.VMEM((length, dim), jnp.float32),
            pltpu.VMEM((length, dim), jnp.float32),
        ],
        compiler_params=pltpu.CompilerParams(dimension_semantics=("arbitrary",)),
        cost_estimate=pl.CostEstimate(
            flops=10 * work * dim, transcendentals=work, bytes_accessed=6 * blocks * dim * width
        ),
    )(pairs, rays)


def local(
    section_tokens,
    enc_ln1,
    enc_qkv,
    enc_out,
    enc_ln2,
    enc_up,
    enc_down,
    set_latent,
    ray_queries,
    dec_query,
    dec_kv,
    dec_out,
    feature_grad,
):
    tokens = section_tokens[0, 0]
    width = tokens.shape[1]
    head_dim = width // HEADS
    local_width = enc_out.shape[1]
    sections = lax.axis_size("section")
    rays = lax.axis_size("ray")
    latent = set_latent[0]
    queries = ray_queries[0]
    cotangent = feature_grad[0]
    f32, bf16 = jnp.float32, jnp.bfloat16

    share = dec_query.shape[0]
    both = jnp.concatenate([dec_query, dec_out], 1)
    w_both = lax.all_gather(both, "section", axis=0, tiled=True)
    w_query, w_mix = w_both[:, :width], w_both[:, width:]
    dec_kv = after(dec_kv, both)
    kv_rows = dec_kv.reshape(share, 2, HEADS, head_dim).transpose(0, 2, 1, 3)
    kv_rows = kv_rows.reshape(share, HEADS, 2 * head_dim)
    by_head = kv_rows.transpose(1, 0, 2)
    w_head = exchange(by_head, "section").reshape(width, 2 * head_dim)
    normed = layer_norm(after(tokens, by_head), enc_ln1[0]).astype(bf16)
    own_pairs = jnp.dot(after(latent, normed), w_head, preferred_element_type=f32).astype(bf16)
    pairs = gather_small(own_pairs, "ray").reshape(-1, 2 * head_dim)

    packed = jnp.dot(
        after(lax.all_gather(normed, "ray", axis=0, tiled=True), pairs),
        enc_qkv[0].reshape(width, 3 * local_width),
        preferred_element_type=f32,
    ).astype(bf16)
    mixed = attend_heads(packed, head_dim)
    attn_parts = jnp.dot(mixed, enc_out[0], preferred_element_type=f32).astype(bf16)
    attn_rows = lax.psum_scatter(attn_parts, "ray", scatter_dimension=0, tiled=True)

    queries = after(queries, attn_parts)
    query_t = lax.dot_general(w_query, queries, (((0,), (1,)), ((), ())), preferred_element_type=f32)
    grad_t = lax.dot_general(w_mix, cotangent, NT, preferred_element_type=f32)
    rows = queries.shape[0]
    packed_rays = jnp.concatenate(
        [
            query_t.astype(bf16).reshape(HEADS, head_dim, rows),
            grad_t.astype(bf16).reshape(HEADS, head_dim, rows),
        ],
        1,
    )
    attn_rows = after(attn_rows, packed_rays).astype(f32)
    hidden = (tokens.astype(f32) + attn_rows).astype(bf16)
    normed_two = layer_norm(hidden, enc_ln2[0]).astype(bf16)
    mixed_t, pair_grad = attend_rays(pairs, after(exchange(packed_rays, "section"), normed_two))
    attended_t = exchange(mixed_t, "section").reshape(width, rows)
    mix_term = jnp.dot(attended_t, cotangent, preferred_element_type=f32).astype(bf16)
    term = lax.psum_scatter(mix_term, "ray", scatter_dimension=0, tiled=True)
    upper = jax.nn.gelu(
        jnp.dot(
            after(lax.all_gather(normed_two, "ray", axis=0, tiled=True), mix_term),
            enc_up[0],
            preferred_element_type=f32,
        ),
        approximate=True,
    ).astype(bf16)
    lower_parts = jnp.dot(upper, enc_down[0], preferred_element_type=f32).astype(bf16)
    lower_rows = lax.psum_scatter(lower_parts, "ray", scatter_dimension=0, tiled=True).astype(f32)
    pair_grad, attended_t = lax.optimization_barrier((pair_grad, attended_t, lower_parts))[:2]
    features = (
        queries.astype(f32) + lax.dot_general(attended_t, w_mix, TN, preferred_element_type=f32)
    ).astype(bf16)

    count = latent.shape[0]
    pair_sum = jnp.sum(
        exchange(pair_grad.reshape(rays, count, 2 * head_dim), "ray").astype(f32), 0
    ).astype(bf16)
    latent_part = lax.dot_general(pair_sum, w_head, NT, preferred_element_type=f32).astype(bf16)
    latent_part = exchange(after(latent_part, features).reshape(sections, -1, width), "section")
    latent_rows = jnp.sum(latent_part.astype(f32), 0).astype(bf16)

    term = after(term, latent_rows)
    term = jnp.sum(exchange(term.reshape(sections, -1, width), "section").astype(f32), 0)
    term = term + lax.ppermute(term, "dp", [(0, 1), (1, 0)])
    term = gather_small(term.astype(bf16), "section").reshape(-1, width)
    out_grad = lax.all_gather(term, "ray", axis=0, tiled=True).astype(f32)
    latent_grad = gather_small(after(latent_rows, term), "section").reshape(count, width)

    layer_out = (hidden.astype(f32) + lower_rows).astype(bf16)
    handed = shifted(layer_out, "section", 1)
    columns = width // sections
    layer_out = after(layer_out, latent_grad)
    finished = exchange(layer_out.T.reshape(sections, columns, count), "section")[sections - 1].T
    return (handed[None, None], finished[None], features[None], latent_grad[None], out_grad)


def solution(mesh):
    return jax.shard_map(
        local,
        mesh=mesh,
        in_specs=(
            P("section", "dp", "ray", None),
            P("section", None),
            P("section", None, None, "ray"),
            P("section", "ray", None),
            P("section", None),
            P("section", None, "ray"),
            P("section", "ray", None),
            P("dp", "ray", None),
            P("dp", ("section", "ray"), None),
            P("section", None),
            P("section", None, None),
            P("section", None),
            P("dp", ("section", "ray"), None),
        ),
        out_specs=(
            P("section", "dp", "ray", None),
            P("dp", "ray", "section"),
            P("dp", ("section", "ray"), None),
            P("dp", "ray", None),
            P(),
        ),
        check_vma=False,
    )
```

time: 929 us -> 385 us (0.41)
  waiting for transfers between devices: 738 us -> 179 us
  matrix products: 112 us -> 28.2 us
  blocking collectives: 0 us -> 76.7 us
  local copies, waits for them, and re-layouts: 49.6 us -> 10.7 us
  starting transfers between devices: 2.78 us -> 36.7 us
  Pallas kernels: 0 us -> 29.4 us
    psum x2 -> x0, waiting for transfers between devices: 382 us -> none  [the longest x1 273 us: local(): out_grad = lax.psum(mix_term, ('section', 'ray', 'dp'))]
    all_gather x5 -> x3, waiting for transfers between devices: 215 us -> 73.7 us  [the longest x1 49.1 us: local(): w_both = lax.all_gather(both, 'section', axis=0, tiled=True)]
    all_to_all x0 -> x5, blocking collectives: none -> 76.7 us  [exchange(): return lax.all_to_all(blocks, axis, split_axis=0, concat_axis=0, tiled=True)]
    dot_general x14 -> x9, matrix products: 92.9 us -> 19 us  [the longest x1 5.52 us: local(): jnp.dot(upper, enc_down[0], preferred_element_type=f32).astype(bf16)]
    unnamed x12 -> x7, waiting for transfers between devices: 53.9 us -> 0.78 us
    all_to_all x0 -> x5, waiting for transfers between devices: none -> 39.3 us  [exchange(): return lax.all_to_all(blocks, axis, split_axis=0, concat_axis=0, tiled=True)]
    all_gather x1, waiting for transfers between devices: 42.5 us -> 7.4 us  [local(): lax.all_gather(normed, 'ray', axis=0, tiled=True)]
    all_to_all x0 -> x5, starting transfers between devices: none -> 33.4 us  [exchange(): return lax.all_to_all(blocks, axis, split_axis=0, concat_axis=0, tiled=True)]
  transfers between devices with their start and end apart: 12 -> 14, of which waited for: 11 -> 12; matrix products, arithmetic and copies ran while one was open for 16% -> 9% of each run, Pallas kernels for 0% -> 8%
where the time goes in v1:
time: 385 us; the launch traced here: 384 us
  waiting for transfers between devices  179 us (46%)
  blocking collectives  76.7 us (20%)
  starting transfers between devices  36.7 us (10%)
  Pallas kernels  29.4 us (8%)
  matrix products  28.2 us (7%)
  between operations  14.4 us (4%)
  local copies, waits for them, and re-layouts  10.7 us (3%)
  other arithmetic  8.84 us (2%)
    all_to_all x5, blocking collectives, exchange(): return lax.all_to_all(blocks, axis, split_axis=0, concat_axis=0, tiled=True)  76.7 us
    all_gather x1, waiting for transfers between devices, local(): w_both = lax.all_gather(both, 'section', axis=0, tiled=True)  49.1 us
    reduce_scatter x1, waiting for transfers between devices, local(): lax.psum_scatter(attn_parts, 'ray', scatter_dimension=0, tiled=True)  41.1 us
    all_to_all x5, waiting for transfers between devices, exchange(): return lax.all_to_all(blocks, axis, split_axis=0, concat_axis=0, tiled=True)  39.3 us
    all_to_all x5, starting transfers between devices, exchange(): return lax.all_to_all(blocks, axis, split_axis=0, concat_axis=0, tiled=True)  33.4 us
    pallas_call x1, Pallas kernels, attend_rays(): pl.pallas_call(head_kernel, grid=(blocks,), in_specs=[pl.BlockSpec((lengt...  29.4 us
    all_gather x1, waiting for transfers between devices, local(): out_grad = lax.all_gather(term, 'ray', axis=0, tiled=True).astype(f32)  24.6 us
    reduce_scatter x1, waiting for transfers between devices, local(): lax.psum_scatter(lower_parts, 'ray', scatter_dimension=0, tiled=True)  8.67 us
  transfers between devices with their start and end apart: 14, of which 12 were waited for; matrix products, arithmetic and copies ran while one was open for 9% of the time, Pallas kernels for 8%

profile of v1, /device:TPU:2, one launch (start us, length us, event | category | flops | bytes accessed | tf_op | source)
XLA Modules:
  0.0 383.7 jit_solution(16260188463796728731)
XLA Ops:
  7.2 1.0 constant_dynamic-update-slice_fusion.1
  8.3 0.9 constant_dynamic-update-slice_fusion
  9.2 1.4 reshape.82
  10.6 0.4 copy.32
  11.0 0.2 reshape.83
  11.3 0.1 convert_reduce_fusion.1
  11.4 0.2 fusion.54
  11.7 0.9 fusion.56
  12.7 0.7 all-gather.7.cloned.1.call-update
  13.4 0.8 copy.26
  14.2 7.5 %all-to-all-start = ((bf16[16,64,128]{2,1,0:T(8,128)(2,1)}), bf16[16,64,128]{2,1,0:T(8,128)(2,1)S(1)}, u32[]{:S(2)}, u32[]{:S(2)}) async-start(bf16[16,64,128]{2,1,0:T(8,128)(2,1)} %copy.26), calls=%async_computation | async-start | bytes 524288 | tf_op jit(solution)/shard_map/all_to_all | solution.py:45
  21.6 6.9 %all-to-all-done = bf16[16,64,128]{2,1,0:T(8,128)(2,1)S(1)} async-done(((bf16[16,64,128]{2,1,0:T(8,128)(2,1)}), bf16[16,64,128]{2,1,0:T(8,128)(2,1)S(1)}, u32[]{:S(2)}, u32[]{:S(2)}) %all-to-all-start) | async-done | bytes 262176 | tf_op jit(solution)/shard_map/all_to_all | solution.py:45
  28.5 0.2 convolution_convert_fusion.5
  28.7 0.7 broadcast_in_dim.12
  29.5 8.5 %all-to-all-start.1 = ((bf16[8,128,128]{2,1,0:T(8,128)(2,1)}), bf16[8,128,128]{2,1,0:T(8,128)(2,1)S(1)}, u32[]{:S(2)}, u32[]{:S(2)}) async-start(bf16[8,128,128]{2,1,0:T(8,128)(2,1)} %broadcast_in_dim.12), calls=%async_computation.1 | async-start | bytes 524288 | tf_op jit(solution)/shard_map/all_to_all | solution.py:45
  38.0 0.3 copy.27
  38.3 15.4 %all-to-all-done.1 = bf16[8,128,128]{2,1,0:T(8,128)(2,1)S(1)} async-done(((bf16[8,128,128]{2,1,0:T(8,128)(2,1)}), bf16[8,128,128]{2,1,0:T(8,128)(2,1)S(1)}, u32[]{:S(2)}, u32[]{:S(2)}) %all-to-all-start.1) | async-done | bytes 262176 | tf_op jit(solution)/shard_map/all_to_all | solution.py:45
  53.7 7.4 %all-gather.5.cloned.1.call-done = bf16[1024,1024]{1,0:T(8,128)(2,1)} async-done(((bf16[128,1024]{1,0:T(8,128)(2,1)}), bf16[1024,1024]{1,0:T(8,128)(2,1)}) %all-gather.5.cloned.1.call-update) | async-done | bytes 2097168 | tf_op jit(solution)/shard_map/all_gather | solution.py:170
  61.1 2.6 convolution_convert_fusion.3
  63.7 4.9 %fusion.67 = (f32[2,1024]{1,0:T(2,128)S(1)}, f32[2,1024,1024]{1,2,0:T(8,128)}) fusion(bf16[1024,3,2,64]{0,3,2,1:T(8,128)(2,1)S(1)} %bitcast.115), kind=kOutput, calls=%fused_computation.81 | convolution fusion | flops 274727936 | bytes 8921088 | tf_op jit(solution)/shard_map/sub | solution.py:28
  68.6 4.3 %fusion.32 = bf16[2,64,1024]{2,1,0:T(8,128)(2,1)S(1)} fusion(f32[2,1024,1024]{1,2,0:T(8,128)} %get-tuple-element.38, f32[2,1024]{1,0:T(2,128)S(1)} %get-tuple-element.37, bf16[1024,3,2,64]{0,3,2,1:T(8,128)(2,1)S(1)} %bitcast.116), kind=kOutput, calls=%fused_computation.31 | convolution fusion | flops 272760832 | bytes 8921088 | tf_op jit(solution)/shard_map/hqk,khd->qhd/dot_general | solution.py:40
  72.9 2.1 convolution_convert_fusion.2
  74.9 0.0 all-gather.9.cloned.1.call-start
  75.0 49.1 %all-gather.7.cloned.1.call-done = bf16[1024,2048]{1,0:T(8,128)(2,1)} async-done(((bf16[64,2048]{1,0:T(8,128)(2,1)}), bf16[1024,2048]{1,0:T(8,128)(2,1)}) %all-gather.7.cloned.1.call-update) | async-done | bytes 4194320 | tf_op jit(solution)/shard_map/all_gather | solution.py:158
  124.2 2.5 fusion.26
  126.7 0.3 copy-done.10
  127.0 0.7 fusion.23
  127.7 0.1 pad_maximum_fusion
  127.8 41.1 %reduce-scatter.4.cloned.1.call-done = bf16[128,1024]{1,0:T(8,128)(2,1)} async-done(((bf16[1024,1024]{1,0:T(8,128)(2,1)}), bf16[128,1024]{1,0:T(8,128)(2,1)}) %reduce-scatter.4.cloned.1.call-update) | async-done | bytes 262160 | tf_op jit(solution)/shard_map/reduce_scatter | solution.py:176
  168.9 1.1 convert_reduce_fusion
  170.0 0.2 fusion.51
  170.3 0.9 fusion.53
  171.2 0.0 reduce-scatter.8.cloned.1.call-start
  171.3 21.7 %all_to_all.50.rays_ref = bf16[16,128,256]{2,1,0:T(8,128)(2,1)} all-to-all(bf16[16,128,256]{2,1,0:T(8,128)(2,1)S(1)} %pad_maximum_fusion), channel_id=1, replica_groups=mesh['section'=16,'ray'=8,'dp'=2] {'section'}, dimensions={0} | all-to-all | bytes 2097152 | tf_op jit(solution)/shard_map/all_to_all | solution.py:45
  193.0 29.4 %shard_map.164 = (bf16[16,64,256]{2,1,0:T(8,128)(2,1)}, bf16[1024,128]{1,0:T(8,128)(2,1)}) custom-call(bf16[1024,128]{1,0:T(8,128)(2,1)} %bitcast.108, bf16[16,128,256]{2,1,0:T(8,128)(2,1)} %all_to_all.50.rays_ref), custom_call_target="tpu_custom_call" | custom-call | flops 2684354560 | bytes 1572864 | tf_op jit(solution)/shard_map/pallas_call | solution.py:101
  222.4 15.8 %all_to_all.51 = bf16[16,64,256]{2,1,0:T(8,128)(2,1)S(1)} all-to-all(bf16[16,64,256]{2,1,0:T(8,128)(2,1)} %get-tuple-element.27), channel_id=1, replica_groups=mesh['section'=16,'ray'=8,'dp'=2] {'section'}, dimensions={0} | all-to-all | bytes 1048576 | tf_op jit(solution)/shard_map/all_to_all | solution.py:45
  238.2 2.0 convolution_convert_fusion.1
  240.3 0.2 reduce-scatter.6.cloned.1.call-start
  240.6 0.9 copy-done.11
  241.5 5.5 %convolution_convert_fusion = bf16[1024,1024]{1,0:T(8,128)(2,1)} fusion(bf16[1,512,1024]{2,1,0:T(8,128)(2,1)S(1)} %copy-done, bf16[1024,1024]{1,0:T(8,128)(2,1)} %all-gather.9.cloned.1.call-done, bf16[1,1024,512]{2,1,0:T(8,128)(2,1)S(1)} %copy-done.11), kind=kOutput, calls=%fused_computation.18 | convolution fusion | flops 2153250816 | bytes 6291456 | tf_op jit(solution)/shard_map/dot_general | solution.py:204
  247.0 4.4 %all-to-all-start.5 = ((bf16[8,128,128]{2,1,0:T(8,128)(2,1)}), bf16[8,128,128]{2,1,0:T(8,128)(2,1)S(1)}, u32[]{:S(2)}, u32[]{:S(2)}) async-start(bf16[8,128,128]{2,1,0:T(8,128)(2,1)} %bitcast.30), calls=%async_computation.7 | async-start | bytes 524288 | tf_op jit(solution)/shard_map/all_to_all | solution.py:45
  251.5 3.1 fusion.29
  254.6 12.1 %all-to-all-done.5 = bf16[8,128,128]{2,1,0:T(8,128)(2,1)S(1)} async-done(((bf16[8,128,128]{2,1,0:T(8,128)(2,1)}), bf16[8,128,128]{2,1,0:T(8,128)(2,1)S(1)}, u32[]{:S(2)}, u32[]{:S(2)}) %all-to-all-start.5) | async-done | bytes 262176 | tf_op jit(solution)/shard_map/all_to_all | solution.py:45
  266.8 0.2 convolution_convert_fusion.4
  267.1 13.1 %all_to_all.52 = bf16[16,8,1024]{2,1,0:T(8,128)(2,1)S(1)} all-to-all(bf16[16,8,1024]{2,1,0:T(8,128)(2,1)S(1)} %bitcast.102), channel_id=1, replica_groups=mesh['section'=16,'ray'=8,'dp'=2] {'section'}, dimensions={0} | all-to-all | bytes 524288 | tf_op jit(solution)/shard_map/all_to_all | solution.py:45
  280.2 4.1 %reduce-scatter.8.cloned.1.call-done = bf16[128,1024]{1,0:T(8,128)(2,1)} async-done(((bf16[1024,1024]{1,0:T(8,128)(2,1)}), bf16[128,1024]{1,0:T(8,128)(2,1)}) %reduce-scatter.8.cloned.1.call-update) | async-done | bytes 262160 | tf_op jit(solution)/shard_map/reduce_scatter | solution.py:195
  284.3 13.8 %all_to_all.53 = bf16[16,8,1024]{2,1,0:T(8,128)(2,1)S(1)} all-to-all(bf16[16,8,1024]{2,1,0:T(8,128)(2,1)} %bitcast.109), channel_id=1, replica_groups=mesh['section'=16,'ray'=8,'dp'=2] {'section'}, dimensions={0} | all-to-all | bytes 524288 | tf_op jit(solution)/shard_map/all_to_all | solution.py:45
  298.1 0.8 collective-permute-start.1
  299.0 3.4 collective-permute-done.1
  302.4 12.4 %all_to_all.54 = bf16[16,8,1024]{2,1,0:T(8,128)(2,1)} all-to-all(bf16[16,8,1024]{2,1,0:T(8,128)(2,1)S(1)} %broadcast_in_dim.16), channel_id=1, replica_groups=mesh['section'=16,'ray'=8,'dp'=2] {'section'}, dimensions={0} | all-to-all | bytes 524288 | tf_op jit(solution)/shard_map/all_to_all | solution.py:45
  314.8 0.7 broadcast_in_dim.17
  315.5 5.9 %all-to-all-start.9 = ((bf16[16,8,1024]{2,1,0:T(8,128)(2,1)}), bf16[16,8,1024]{2,1,0:T(8,128)(2,1)S(1)}, u32[]{:S(2)}, u32[]{:S(2)}) async-start(bf16[16,8,1024]{2,1,0:T(8,128)(2,1)} %broadcast_in_dim.17), calls=%async_computation.12 | async-start | bytes 524288 | tf_op jit(solution)/shard_map/all_to_all | solution.py:45
  321.4 8.7 %reduce-scatter.6.cloned.1.call-done = bf16[128,1024]{1,0:T(8,128)(2,1)} async-done(((bf16[1024,1024]{1,0:T(8,128)(2,1)}), bf16[128,1024]{1,0:T(8,128)(2,1)}) %reduce-scatter.6.cloned.1.call-update) | async-done | bytes 262160 | tf_op jit(solution)/shard_map/reduce_scatter | solution.py:205
  330.1 1.0 fusion.57
  331.1 0.8 copy.29
  332.0 7.1 %all-to-all-start.4 = ((bf16[16,64,128]{2,1,0:T(8,128)(2,1)}), bf16[16,64,128]{2,1,0:T(8,128)(2,1)S(1)}, u32[]{:S(2)}, u32[]{:S(2)}) async-start(bf16[16,64,128]{2,1,0:T(8,128)(2,1)} %bitcast.25), calls=%async_computation.6 | async-start | bytes 524288 | tf_op jit(solution)/shard_map/all_to_all | solution.py:45
  339.1 2.0 collective-permute-start
  341.1 4.9 %all-to-all-done.4 = bf16[16,64,128]{2,1,0:T(8,128)(2,1)S(1)} async-done(((bf16[16,64,128]{2,1,0:T(8,128)(2,1)}), bf16[16,64,128]{2,1,0:T(8,128)(2,1)S(1)}, u32[]{:S(2)}, u32[]{:S(2)}) %all-to-all-start.4) | async-done | bytes 262176 | tf_op jit(solution)/shard_map/all_to_all | solution.py:45
  346.0 0.6 slice_bitcast_fusion.14
  346.6 0.2 collective-permute-done
  346.8 24.6 %all-gather.11.cloned.1.call-done = bf16[1024,1024]{1,0:T(8,128)(2,1)} async-done(((bf16[128,1024]{1,0:T(8,128)(2,1)}), bf16[1024,1024]{1,0:T(8,128)(2,1)}) %all-gather.11.cloned.1.call-update) | async-done | bytes 2097168 | tf_op jit(solution)/shard_map/all_gather | solution.py:223
  371.4 4.1 %convert_element_type.108 = f32[1024,1024]{1,0:T(8,128)} convert(bf16[1024,1024]{1,0:T(8,128)(2,1)} %all-gather.11.cloned.1.call-done) | non-fusion elementwise | flops 1048576 | bytes 6291456 | tf_op jit(solution)/shard_map/convert_element_type | solution.py:223
  375.4 0.7 copy.36
  376.1 0.7 copy.37
  (47 shorter events, 0.5 us)
Async XLA Ops:
  7.2 233.4 %copy-start = (bf16[1,512,1024]{2,1,0:T(8,128)(2,1)S(1)}, bf16[1,512,1024]{2,1,0:T(8,128)(2,1)}, u32[]{:S(2)}) copy-start(bf16[1,512,1024]{2,1,0:T(8,128)(2,1)} %param.19) | copy-start | bytes 3145732
  7.2 4.1 %copy-start.1 = (bf16[1,1,128,1024]{3,2,1,0:T(8,128)(2,1)S(1)}, bf16[1,1,128,1024]{3,2,1,0:T(8,128)(2,1)}, u32[]{:S(2)}) copy-start(bf16[1,1,128,1024]{3,2,1,0:T(8,128)(2,1)} %param.13) | copy-start | bytes 786436
  7.2 4.5 %copy-start.8 = (f32[1,1024]{1,0:T(1,128)S(1)}, f32[1,1024]{1,0:T(1,128)}, u32[]{:S(2)}) copy-start(f32[1,1024]{1,0:T(1,128)} %param.14) | copy-start | bytes 12292
  7.2 53.9 %all-gather.5.cloned.1.call-start = ((), (), s32[]{:S(2)}) async-start(), calls=%async_computation.13 | async-start | bytes 2359296 | tf_op jit(solution)/shard_map/all_gather | solution.py:170
  9.2 3.5 copy-start.3
  10.6 17.9 %copy-start.6 = (bf16[1,128,1024]{2,1,0:T(8,128)(2,1)S(1)}, bf16[1,128,1024]{2,1,0:T(8,128)(2,1)}, u32[]{:S(2)}) copy-start(bf16[1,128,1024]{2,1,0:T(8,128)(2,1)} %param.20) | copy-start | bytes 786436
  11.3 26.7 %copy-start.2 = (bf16[1,1024,3,128]{3,1,2,0:T(8,128)(2,1)S(1)}, bf16[1,1024,3,128]{3,1,2,0:T(8,128)(2,1)}, u32[]{:S(2)}) copy-start(bf16[1,1024,3,128]{3,1,2,0:T(8,128)(2,1)} %param.15) | copy-start | bytes 2359300
  12.6 111.5 %all-gather.7.cloned.1.call-start = ((), (), s32[]{:S(2)}) async-start(), calls=%async_computation.15 | async-start | bytes 4456448 | tf_op jit(solution)/shard_map/all_gather | solution.py:158
  14.2 14.4 %all-to-all-start = ((bf16[16,64,128]{2,1,0:T(8,128)(2,1)}), bf16[16,64,128]{2,1,0:T(8,128)(2,1)S(1)}, u32[]{:S(2)}, u32[]{:S(2)}) async-start(bf16[16,64,128]{2,1,0:T(8,128)(2,1)} %copy.26), calls=%async_computation | async-start | bytes 524288 | tf_op jit(solution)/shard_map/all_to_all | solution.py:45
  29.5 24.2 %all-to-all-start.1 = ((bf16[8,128,128]{2,1,0:T(8,128)(2,1)}), bf16[8,128,128]{2,1,0:T(8,128)(2,1)S(1)}, u32[]{:S(2)}, u32[]{:S(2)}) async-start(bf16[8,128,128]{2,1,0:T(8,128)(2,1)} %broadcast_in_dim.12), calls=%async_computation.1 | async-start | bytes 524288 | tf_op jit(solution)/shard_map/all_to_all | solution.py:45
  38.0 131.0 %reduce-scatter.4.cloned.1.call-start = ((), (), s32[]{:S(2)}) async-start(), calls=%async_computation.14 | async-start | bytes 2359296 | tf_op jit(solution)/shard_map/reduce_scatter | solution.py:176
  53.7 10.0 %copy-start.7 = (bf16[8,128,128]{2,1,0:T(8,128)(2,1)}, bf16[8,128,128]{2,1,0:T(8,128)(2,1)S(1)}, u32[]{:S(2)}) copy-start(bf16[8,128,128]{2,1,0:T(8,128)(2,1)S(1)} %all-to-all-done.1) | copy-start | bytes 786436
  68.6 4.3 %copy-start.5 = (bf16[1,128,1024]{2,1,0:T(8,128)(2,1)S(1)}, bf16[1,128,1024]{2,1,0:T(8,128)(2,1)}, u32[]{:S(2)}) copy-start(bf16[1,128,1024]{2,1,0:T(8,128)(2,1)} %param.16) | copy-start | bytes 786436
  72.9 51.3 %copy-start.12 = (bf16[1,256,1024]{2,1,0:T(8,128)(2,1)S(1)}, bf16[1,256,1024]{2,1,0:T(8,128)(2,1)}, u32[]{:S(2)}) copy-start(bf16[1,256,1024]{2,1,0:T(8,128)(2,1)} %param.21) | copy-start | bytes 1572868
  74.9 165.6 %all-gather.9.cloned.1.call-start = ((), (), s32[]{:S(2)}) async-start(), calls=%async_computation.16 | async-start | bytes 2359296 | tf_op jit(solution)/shard_map/all_gather | solution.py:198
  75.0 51.7 %copy-start.4 = (bf16[1,256,1024]{2,1,0:T(8,128)(2,1)S(1)}, bf16[1,256,1024]{2,1,0:T(8,128)(2,1)}, u32[]{:S(2)}) copy-start(bf16[1,256,1024]{2,1,0:T(8,128)(2,1)} %param.25) | copy-start | bytes 1572868
  124.2 2.8 copy-start.10
  127.7 42.5 %copy-start.9 = (f32[1,1024]{1,0:T(1,128)S(1)}, f32[1,1024]{1,0:T(1,128)}, u32[]{:S(2)}) copy-start(f32[1,1024]{1,0:T(1,128)} %param.17) | copy-start | bytes 12292
  171.2 113.1 %reduce-scatter.8.cloned.1.call-start = ((), (), s32[]{:S(2)}) async-start(), calls=%async_computation.18 | async-start | bytes 2359296 | tf_op jit(solution)/shard_map/reduce_scatter | solution.py:195
  240.3 1.2 copy-start.11
  240.3 89.8 %reduce-scatter.6.cloned.1.call-start = ((), (), s32[]{:S(2)}) async-start(), calls=%async_computation.17 | async-start | bytes 2359296 | tf_op jit(solution)/shard_map/reduce_scatter | solution.py:205
  247.0 4.5 %copy-start.13 = (bf16[1,256,1024]{2,1,0:T(8,128)(2,1)S(1)}, bf16[1,256,1024]{2,1,0:T(8,128)(2,1)}, u32[]{:S(2)}) copy-start(bf16[1,256,1024]{2,1,0:T(8,128)(2,1)} %param.21) | copy-start | bytes 1572868
  247.0 19.8 %all-to-all-start.5 = ((bf16[8,128,128]{2,1,0:T(8,128)(2,1)}), bf16[8,128,128]{2,1,0:T(8,128)(2,1)S(1)}, u32[]{:S(2)}, u32[]{:S(2)}) async-start(bf16[8,128,128]{2,1,0:T(8,128)(2,1)} %bitcast.30), calls=%async_computation.7 | async-start | bytes 524288 | tf_op jit(solution)/shard_map/all_to_all | solution.py:45
  251.5 119.9 %all-gather.11.cloned.1.call-start = ((), (), s32[]{:S(2)}) async-start(), calls=%async_computation.19 | async-start | bytes 2359296 | tf_op jit(solution)/shard_map/all_gather | solution.py:223
  298.1 4.2 %collective-permute-start.1 = (f32[8,1024]{1,0:T(8,128)S(1)}, f32[8,1024]{1,0:T(8,128)S(1)}, u32[]{:S(2)}, u32[]{:S(2)}) collective-permute-start(f32[8,1024]{1,0:T(8,128)S(1)} %convert_reduce_fusion.2), channel_id=1, source_target_pairs={{0,1},{1,0},{2,3},{3,2},{4,5},{5,4},{6,7},{7,6},{8,9},{9,8},{10,11... | collective-permute-start | bytes 98312 | tf_op jit(solution)/shard_map/ppermute | solution.py:221
  315.5 16.4 %all-to-all-start.9 = ((bf16[16,8,1024]{2,1,0:T(8,128)(2,1)}), bf16[16,8,1024]{2,1,0:T(8,128)(2,1)S(1)}, u32[]{:S(2)}, u32[]{:S(2)}) async-start(bf16[16,8,1024]{2,1,0:T(8,128)(2,1)} %broadcast_in_dim.17), calls=%async_computation.12 | async-start | bytes 524288 | tf_op jit(solution)/shard_map/all_to_all | solution.py:45
  332.0 14.0 %all-to-all-start.4 = ((bf16[16,64,128]{2,1,0:T(8,128)(2,1)}), bf16[16,64,128]{2,1,0:T(8,128)(2,1)S(1)}, u32[]{:S(2)}, u32[]{:S(2)}) async-start(bf16[16,64,128]{2,1,0:T(8,128)(2,1)} %bitcast.25), calls=%async_computation.6 | async-start | bytes 524288 | tf_op jit(solution)/shard_map/all_to_all | solution.py:45
  339.1 7.7 %collective-permute-start = (bf16[128,1024]{1,0:T(8,128)(2,1)S(1)}, bf16[128,1024]{1,0:T(8,128)(2,1)S(1)}, u32[]{:S(2)}, u32[]{:S(2)}) collective-permute-start(bf16[128,1024]{1,0:T(8,128)(2,1)S(1)} %fusion.57), channel_id=1, source_target_pairs={{0,16},{16,32},{32,48},{48,64},{64,80},{80,96},{96,112},{112,128},... | collective-permute-start | bytes 786440 | tf_op jit(solution)/shard_map/ppermute | solution.py:16
Sparse Core Ops, SparseCore 0:
  12.8 48.2 all-gather.4
  64.4 59.7 all-gather.6
  127.3 41.5 reduce-scatter.3
  171.3 39.8 all-gather.8
  240.4 43.8 reduce-scatter.7
  287.3 42.7 reduce-scatter.5
  331.9 39.4 all-gather.10
